TPU v7x, 32 devices: a whole 2x2x4 slice. The times are simulated.
32 devices in a mesh: seq: 8 (over z, x), head: 4 (over y, core).
Axes of the slice: x: 2, y: 2, z: 4, core: 2. Of those that a mesh axis runs over, the one named last changes fastest.
Arguments:
- queries: bfloat16 [2, 8, 14336], P(None, 'seq', 'head'), may hold values from -150 to 150
- new_keys: bfloat16 [2, 8, 14336], P(None, 'seq', 'head'), may hold values from -6 to 6
- new_values: bfloat16 [2, 8, 14336], P(None, 'seq', 'head'), may hold values from -6 to 6
- cache_keys: bfloat16 [8192, 14336], P('seq', 'head'), may hold values from -6 to 6
- cache_values: bfloat16 [8192, 14336], P('seq', 'head'), may hold values from -6 to 6
- slopes: float32 [112], P('head'), may hold values from 7.324219e-05 to 0.025
- seg_blocks: int32 [8], replicated, may hold values from 1 to 32, 48 in all
- request_row: int32 [8], replicated, may hold values from 0 to 7, each once
- out_weight: bfloat16 [14336, 14336], P('head', 'seq'), may hold values from -0.046875 to 0.046875
- residual: bfloat16 [2, 8, 14336], P(None, 'head', 'seq'), may hold values from -6 to 6
Outputs:
- mixed: bfloat16 [2, 8, 14336], P(None, 'head', 'seq')
Inputs may be any that keep to these rules, and one draw needn't show every extreme that they name: `seg_blocks`: the requests are packed in order from block 0; 48 blocks are used and the rest of the cache is unused. `request_row`: each query row belongs to exactly one request.
All inputs are finite; a program needn't handle non-finite values.
Results may differ from a plain program's by a relative error of at most 0.006.
Values may be sent and summed in bfloat16 or wider, within the bound.
A program may use at most 64 MiB of HBM per device.

v0:
```python
import math
import jax
import jax.numpy as jnp
from jax import lax
from jax.sharding import PartitionSpec as P

BLK = 128
NEG = -1e30


def combine(first, second):
    top_a, sum_a, acc_a = first
    top_b, sum_b, acc_b = second
    top = jnp.maximum(top_a, top_b)
    weight_a = jnp.exp(top_a - top)
    weight_b = jnp.exp(top_b - top)
    return (
        top,
        sum_a * weight_a + sum_b * weight_b,
        acc_a * weight_a[..., None] + acc_b * weight_b[..., None],
    )


def self_terms(query, key_new, value_new, slopes, scale):
    query = query.astype(jnp.float32)
    key_new = key_new.astype(jnp.float32)
    value_new = value_new.astype(jnp.float32)
    first = jnp.sum(query[0] * key_new[0], axis=-1) * scale
    cross = jnp.sum(query[1] * key_new[0], axis=-1) * scale - slopes
    second = jnp.sum(query[1] * key_new[1], axis=-1) * scale
    upper = jnp.maximum(cross, second)
    e_cross = jnp.exp(cross - upper)
    e_second = jnp.exp(second - upper)
    top = jnp.stack([first, upper])
    total = jnp.stack([jnp.ones_like(first), e_cross + e_second])
    acc = jnp.stack(
        [value_new[0], e_cross[..., None] * value_new[0] + e_second[..., None] * value_new[1]]
    )
    return (top, total, acc)


def body(
    queries,
    new_keys,
    new_values,
    cache_keys,
    cache_values,
    slopes,
    seg_blocks,
    request_row,
    out_weight,
    residual,
):
    heads = slopes.shape[0]
    width = queries.shape[2]
    hdim = width // heads
    requests = seg_blocks.shape[0]
    own_rows = queries.shape[1]
    blocks = cache_keys.shape[0] // BLK
    scale = 1.0 / math.sqrt(hdim)
    everyone = lax.all_gather(queries, "seq", axis=1, tiled=True)
    place = lax.axis_index("seq")
    starts = jnp.cumsum(seg_blocks) - seg_blocks
    index = place * blocks + jnp.arange(blocks, dtype=jnp.int32)
    hit = (index[:, None] >= starts[None, :]) & (index[:, None] < (starts + seg_blocks)[None, :])
    live = jnp.any(hit, axis=1)
    block_row = jnp.sum(jnp.where(hit, request_row[None, :], 0), axis=1)
    first = jnp.sum(jnp.where(hit, starts[None, :], 0), axis=1)
    length = jnp.sum(jnp.where(hit, seg_blocks[None, :], 0), axis=1)
    base = length * BLK - (index - first) * BLK
    block_query = jnp.take(everyone, block_row, axis=1).reshape(2, blocks, heads, hdim)
    keys = cache_keys.reshape(blocks, BLK, heads, hdim)
    values = cache_values.reshape(blocks, BLK, heads, hdim)
    scores = (
        jnp.einsum("sbhd,bthd->bsht", block_query, keys, preferred_element_type=jnp.float32) * scale
    )
    dist = (
        base[:, None, None]
        + jnp.arange(2, dtype=jnp.int32)[None, :, None]
        - jnp.arange(BLK, dtype=jnp.int32)[None, None, :]
    ).astype(jnp.float32)
    scores = scores - slopes[None, None, :, None] * dist[:, :, None, :]
    top = jnp.max(scores, axis=-1)
    probs = jnp.exp(scores - top[..., None])
    total = jnp.sum(probs, axis=-1)
    acc = jnp.einsum(
        "bsht,bthd->bshd", probs.astype(jnp.bfloat16), values, preferred_element_type=jnp.float32
    )
    top = jnp.where(live[:, None, None], top, NEG)
    total = jnp.where(live[:, None, None], total, 0.0)
    acc = jnp.where(live[:, None, None, None], acc, 0.0)
    rowhot = (block_row[:, None] == jnp.arange(requests, dtype=jnp.int32)[None, :]) & live[:, None]
    tab_top = jnp.max(jnp.where(rowhot[:, :, None, None], top[:, None], NEG), axis=0).transpose(
        1, 0, 2
    )
    ratio = jnp.exp(top - jnp.take(tab_top, block_row, axis=1).transpose(1, 0, 2))
    onehot = rowhot.astype(jnp.float32)
    tab_sum = jnp.einsum("br,bsh->srh", onehot, ratio * total, precision=lax.Precision.HIGHEST)
    tab_acc = jnp.einsum(
        "br,bshd->srhd", onehot, ratio[..., None] * acc, precision=lax.Precision.HIGHEST
    )
    mine = self_terms(
        queries.reshape(2, own_rows, heads, hdim),
        new_keys.reshape(2, own_rows, heads, hdim),
        new_values.reshape(2, own_rows, heads, hdim),
        slopes,
        scale,
    )
    got_top, got_sum, got_acc = (
        lax.all_to_all(tab_top[None], "seq", split_axis=2, concat_axis=0, tiled=True),
        lax.all_to_all(tab_sum[None], "seq", split_axis=2, concat_axis=0, tiled=True),
        lax.all_to_all(tab_acc[None], "seq", split_axis=2, concat_axis=0, tiled=True),
    )
    highest = jnp.max(got_top, axis=0)
    factor = jnp.exp(got_top - highest[None])
    gathered_sum = jnp.sum(got_sum * factor, axis=0)
    gathered_acc = jnp.sum(got_acc * factor[..., None], axis=0)
    top_own, sum_own, acc_own = combine((highest, gathered_sum, gathered_acc), mine)
    attended = (acc_own / sum_own[..., None]).astype(jnp.bfloat16).reshape(2, own_rows, width)
    projected = jnp.einsum(
        "srx,xy->sry",
        lax.all_gather(attended, "seq", axis=1, tiled=True),
        out_weight,
        preferred_element_type=jnp.float32,
    )
    summed = lax.psum_scatter(
        projected.astype(jnp.bfloat16), "head", scatter_dimension=1, tiled=True
    ).astype(jnp.float32)
    return (residual.astype(jnp.float32) + summed).astype(jnp.bfloat16)


def solution(mesh):
    in_specs = (
        P(None, "seq", "head"),
        P(None, "seq", "head"),
        P(None, "seq", "head"),
        P("seq", "head"),
        P("seq", "head"),
        P("head"),
        P(),
        P(),
        P("head", "seq"),
        P(None, "head", "seq"),
    )
    out_specs = P(None, "head", "seq")
    return jax.shard_map(body, mesh=mesh, in_specs=in_specs, out_specs=out_specs, check_vma=False)
```

profile of v0, /device:TPU:0, one launch (start us, length us, event | category | flops | bytes accessed | tf_op | source)
XLA Modules:
  0.0 161.4 jit_solution(8189962348176017590)
XLA Ops:
  0.0 0.0 copy-start.4
  0.0 0.8 reduce-window.8
  0.8 0.7 iota_add_fusion.1
  1.5 0.9 select_reduce_fusion.2
  2.4 0.2 fusion.66
  2.6 32.6 %all_gather.6 = bf16[2,8,3584]{2,0,1:T(2,128)(2,1)S(1)} all-gather(bf16[2,1,3584]{2,0,1:T(2,128)(2,1)} %param.10), channel_id=1, replica_groups=mesh['seq'=8,'head'=4] {'seq'}, dimensions={1}, use_global_device_ids=true | all-gather | bytes 129024 | tf_op jit(solution)/shard_map/all_gather | solution.py:61
  35.2 0.1 iota_add_fusion
  35.3 0.1 subtract_convert_fusion
  35.4 12.9 %reshape.655 = bf16[8,128,28,128]{3,2,1,0:T(8,128)(2,1)} reshape(bf16[1024,3584]{1,0:T(8,128)(2,1)} %param.13) | data formatting | bytes 14680064 | tf_op jit(solution)/shard_map/reshape | solution.py:72
  48.3 0.0 copy-start.1
  48.3 0.8 gather_fusion
  49.1 0.1 bitcast_select_fusion
  49.1 0.0 copy-done.4
  49.2 7.4 %fusion.67 = (f32[8,2,28]{1,2,0:T(8,128)S(1)}, f32[8,2,28,128]{3,1,2,0:T(2,128)S(1)}) fusion(f32[8,2,128]{2,1,0:T(2,128)S(1)} %subtract_convert_fusion, f32[28]{0:T(128)S(1)} %copy-done.4, bf16[8,128,28,128]{3,2,1,0:T(8,128)(2,1)} %reshape.655, bf16[2,8,28,128]{3,1,2,0:T(8,128)(2,1)S(1)} %bitcast_select_fusion), kind=kOutput, calls=%fused_computation.103 | convolution fusion | flops 14908992 | bytes 7694192 | tf_op jit(solution)/shard_map/sbhd,bthd->bsht/dot_general | solution.py:75
  56.5 0.1 copy.149
  56.7 0.1 broadcast_select_fusion
  56.7 0.1 copy.150
  56.8 0.1 select_reduce_fusion
  56.9 0.6 copy.210
  57.5 5.5 %all-to-all-start.1 = ((f32[1,2,8,28]{3,1,0,2:T(2,128)}), f32[1,2,8,28]{3,1,0,2:T(2,128)S(1)}, u32[]{:S(2)}, u32[]{:S(2)}) async-start(f32[1,2,8,28]{3,1,0,2:T(2,128)} %bitcast.107.clone.2), calls=%async_computation.1 | async-start | bytes 16384 | tf_op jit(solution)/shard_map/all_to_all | solution.py:110
  63.0 0.0 copy-done.1
  63.0 1.3 gather_fusion.1
  64.3 0.1 fusion.45
  64.4 0.2 copy.154
  64.5 12.9 %reshape.656 = bf16[8,128,28,128]{3,2,1,0:T(8,128)(2,1)} reshape(bf16[1024,3584]{1,0:T(8,128)(2,1)} %param.14) | data formatting | bytes 14680064 | tf_op jit(solution)/shard_map/reshape | solution.py:73
  77.4 0.0 copy-start.2
  77.4 0.0 copy-start
  77.4 0.0 copy-start.5
  77.4 0.6 fusion.29
  78.0 6.6 %fusion.24 = f32[8,2,28,128]{3,1,2,0:T(2,128)S(1)} fusion(bf16[8,128,28,128]{3,2,1,0:T(8,128)(2,1)} %reshape.656, pred[8]{0:T(512)(128)(4,1)S(1)} %fusion.66, f32[8,2,28,128]{3,1,2,0:T(2,128)S(1)} %get-tuple-element.24, f32[8,2,28]{1,2,0:T(8,128)S(1)} %get-tuple-element.23, f32[8,2,28]{1,2,0:T(8,128)S(1)} %copy.154), kind=kOutput, calls=%fused_computation.16 | convolution fusion | flops 14909440 | bytes 7802376 | tf_op jit(solution)/shard_map/bsht,bthd->bshd/dot_general | solution.py:86
  84.6 0.3 convolution_bitcast_fusion
  84.9 0.1 copy.163
  85.0 0.0 copy-done.2
  85.0 0.1 fusion.40
  85.1 0.1 bitcast_reduce_fusion.2
  85.3 0.0 copy-done
  85.3 0.1 slice_reduce_fusion.1
  85.4 0.1 bitcast_reduce_fusion
  85.5 0.1 fusion.38
  85.6 0.2 convolution_bitcast_fusion.1
  85.8 0.9 copy.158
  86.7 0.6 copy.164
  87.3 0.0 copy-done.5
  87.3 0.6 dynamic-slice
  88.5 0.0 all-to-all-done.1
  88.6 6.0 %all-to-all-start.2 = ((f32[1,2,8,28]{3,1,0,2:T(2,128)}), f32[1,2,8,28]{3,1,0,2:T(2,128)S(1)}, u32[]{:S(2)}, u32[]{:S(2)}) async-start(f32[1,2,8,28]{3,1,0,2:T(2,128)} %copy.164), calls=%async_computation.2 | async-start | bytes 16384 | tf_op jit(solution)/shard_map/all_to_all | solution.py:111
  94.6 0.2 copy.160
  94.8 0.0 copy-start.3
  94.8 6.4 %all-to-all-done.2 = f32[1,2,8,28]{3,1,0,2:T(2,128)S(1)} async-done(((f32[1,2,8,28]{3,1,0,2:T(2,128)}), f32[1,2,8,28]{3,1,0,2:T(2,128)S(1)}, u32[]{:S(2)}, u32[]{:S(2)}) %all-to-all-start.2) | async-done | bytes 1824 | tf_op jit(solution)/shard_map/all_to_all | solution.py:111
  101.2 3.4 %all-to-all-start = ((f32[1,2,8,28,128]{4,1,3,0,2:T(2,128)}), f32[1,2,8,28,128]{4,1,3,0,2:T(2,128)S(1)}, u32[]{:S(2)}, u32[]{:S(2)}) async-start(f32[1,2,8,28,128]{4,1,3,0,2:T(2,128)} %copy.158), calls=%async_computation | async-start | bytes 458752 | tf_op jit(solution)/shard_map/all_to_all | solution.py:112
  104.6 0.1 div.22
  104.8 0.1 mul.264
  104.9 0.1 copy.161
  105.0 7.7 %all-to-all-done = f32[1,2,8,28,128]{4,1,3,0,2:T(2,128)S(1)} async-done(((f32[1,2,8,28,128]{4,1,3,0,2:T(2,128)}), f32[1,2,8,28,128]{4,1,3,0,2:T(2,128)S(1)}, u32[]{:S(2)}, u32[]{:S(2)}) %all-to-all-start) | async-done | bytes 229408 | tf_op jit(solution)/shard_map/all_to_all | solution.py:112
  112.6 0.3 fusion.27
  113.0 0.1 fusion.37
  113.1 30.6 %all_gather.7 = bf16[2,8,3584]{2,0,1:T(2,128)(2,1)S(1)} all-gather(bf16[2,1,3584]{2,0,1:T(2,128)(2,1)S(1)} %fusion.37), channel_id=1, replica_groups=mesh['seq'=8,'head'=4] {'seq'}, dimensions={1}, use_global_device_ids=true | all-gather | bytes 129024 | tf_op jit(solution)/shard_map/all_gather | solution.py:122
  143.6 6.4 %fusion.6 = bf16[2,8,1792]{2,1,0:T(8,128)(2,1)S(1)} fusion(bf16[3584,1792]{1,0:T(8,128)(2,1)} %param.18, bf16[2,8,3584]{2,0,1:T(2,128)(2,1)S(1)} %all_gather.7), kind=kOutput, calls=%fused_computation.8 | convolution fusion | flops 205549568 | bytes 13017088 | tf_op jit(solution)/shard_map/srx,xy->sry/dot_general | solution.py:120
  150.1 10.7 %all-reduce.1 = bf16[2,8,1792]{2,1,0:T(8,128)(2,1)S(1)} all-reduce(bf16[2,8,1792]{2,1,0:T(8,128)(2,1)S(1)} %fusion.6), channel_id=2, replica_groups=mesh['seq'=8,'head'=4] {'head'}, use_global_device_ids=true, to_apply=%region_14.15.clone | all-reduce | flops 28672 | bytes 114688
  160.8 0.0 copy-done.3
  160.8 0.6 add_convert_fusion
  (20 shorter events, 0.3 us)
Async XLA Ops:
  0.0 49.1 %copy-start.4 = (f32[28]{0:T(128)S(1)}, f32[28]{0:T(128)}, u32[]{:S(2)}) copy-start(f32[28]{0:T(128)} %param.15) | copy-start | bytes 340
  48.3 14.7 %copy-start.1 = (bf16[2,1,3584]{2,0,1:T(2,128)(2,1)S(1)}, bf16[2,1,3584]{2,0,1:T(2,128)(2,1)}, u32[]{:S(2)}) copy-start(bf16[2,1,3584]{2,0,1:T(2,128)(2,1)} %param.10) | copy-start | bytes 43012
  57.5 31.0 %all-to-all-start.1 = ((f32[1,2,8,28]{3,1,0,2:T(2,128)}), f32[1,2,8,28]{3,1,0,2:T(2,128)S(1)}, u32[]{:S(2)}, u32[]{:S(2)}) async-start(f32[1,2,8,28]{3,1,0,2:T(2,128)} %bitcast.107.clone.2), calls=%async_computation.1 | async-start | bytes 16384 | tf_op jit(solution)/shard_map/all_to_all | solution.py:110
  77.4 7.6 %copy-start.2 = (bf16[2,1,3584]{2,0,1:T(2,128)(2,1)S(1)}, bf16[2,1,3584]{2,0,1:T(2,128)(2,1)}, u32[]{:S(2)}) copy-start(bf16[2,1,3584]{2,0,1:T(2,128)(2,1)} %param.11) | copy-start | bytes 43012
  77.4 7.8 %copy-start = (bf16[2,1,3584]{2,0,1:T(2,128)(2,1)S(1)}, bf16[2,1,3584]{2,0,1:T(2,128)(2,1)}, u32[]{:S(2)}) copy-start(bf16[2,1,3584]{2,0,1:T(2,128)(2,1)} %param.12) | copy-start | bytes 43012
  77.4 9.9 %copy-start.5 = (u32[32]{0:T(128)S(1)}, u32[32]{0:T(128)}, u32[]{:S(2)}) copy-start(u32[32]{0:T(128)} %constant.63) | copy-start | bytes 388
  88.6 12.6 %all-to-all-start.2 = ((f32[1,2,8,28]{3,1,0,2:T(2,128)}), f32[1,2,8,28]{3,1,0,2:T(2,128)S(1)}, u32[]{:S(2)}, u32[]{:S(2)}) async-start(f32[1,2,8,28]{3,1,0,2:T(2,128)} %copy.164), calls=%async_computation.2 | async-start | bytes 16384 | tf_op jit(solution)/shard_map/all_to_all | solution.py:111
  94.8 66.0 %copy-start.3 = (bf16[2,2,1792]{2,1,0:T(2,128)(2,1)S(1)}, bf16[2,2,1792]{2,1,0:T(2,128)(2,1)}, u32[]{:S(2)}) copy-start(bf16[2,2,1792]{2,1,0:T(2,128)(2,1)} %param.19) | copy-start | bytes 43012
  101.2 11.4 %all-to-all-start = ((f32[1,2,8,28,128]{4,1,3,0,2:T(2,128)}), f32[1,2,8,28,128]{4,1,3,0,2:T(2,128)S(1)}, u32[]{:S(2)}, u32[]{:S(2)}) async-start(f32[1,2,8,28,128]{4,1,3,0,2:T(2,128)} %copy.158), calls=%async_computation | async-start | bytes 458752 | tf_op jit(solution)/shard_map/all_to_all | solution.py:112
where the time goes:
time: 163 us; the launch traced here: 161 us
  blocking collectives  73.9 us (45%)
  local copies, waits for them, and re-layouts  31.6 us (19%)
  matrix products  20.8 us (13%)
  starting transfers between devices  14.9 us (9%)
  waiting for transfers between devices  14.1 us (9%)
  other arithmetic  5.31 us (3%)
    all_gather x1, blocking collectives, body(): everyone = lax.all_gather(queries, 'seq', axis=1, tiled=True)  32.6 us
    all_gather x1, blocking collectives, body(): lax.all_gather(attended, 'seq', axis=1, tiled=True)  30.6 us
    reshape x1, local copies, waits for them, and re-layouts, body(): values = cache_values.reshape(blocks, BLK, heads, hdim)  12.9 us
    reshape x1, local copies, waits for them, and re-layouts, body(): keys = cache_keys.reshape(blocks, BLK, heads, hdim)  12.9 us
    unnamed x1, blocking collectives  10.7 us
    all_to_all x1, waiting for transfers between devices, body(): lax.all_to_all(tab_acc[None], 'seq', split_axis=2, concat_axis=0, tiled=T...  7.65 us
    dot_general x1, matrix products, body(): jnp.einsum('sbhd,bthd->bsht', block_query, keys, preferred_element_type=j...  7.37 us
    dot_general x1, matrix products, body(): jnp.einsum('bsht,bthd->bshd', probs.astype(jnp.bfloat16), values, preferr...  6.58 us
  transfers between devices with their start and end apart: 3, of which 2 were waited for; matrix products, arithmetic and copies ran while one was open for 16% of the time, Pallas kernels for 0%

commit v1 on v0

--- a/solution.py
+++ b/solution.py
@@ -6,6 +6,28 @@
 
 BLK = 128
 NEG = -1e30
+
+
+def in_order(tiles, dim):
+    tiles = jnp.moveaxis(tiles, 0, dim)
+    shape = tiles.shape
+    return tiles.reshape(*shape[:dim], shape[dim] * shape[dim + 1], *shape[dim + 2 :])
+
+
+def collected_by_bits(x, axis):
+    peers = lax.axis_size(axis)
+    blocks = x[None]
+    for level in range(peers.bit_length() - 1):
+        apart = 1 << level
+        other = lax.ppermute(blocks, axis, [(i, i ^ apart) for i in range(peers)])
+        both = jnp.stack([blocks, other])
+        upper = lax.axis_index(axis) >> level & 1
+        blocks = jnp.where(upper == 0, both, both[::-1]).reshape(-1, *x.shape)
+    return blocks
+
+
+def gather_by_bits(shard, axis, dim):
+    return in_order(collected_by_bits(shard, axis), dim)
 
 
 def combine(first, second):
@@ -119,7 +141,7 @@
     attended = (acc_own / sum_own[..., None]).astype(jnp.bfloat16).reshape(2, own_rows, width)
     projected = jnp.einsum(
         "srx,xy->sry",
-        lax.all_gather(attended, "seq", axis=1, tiled=True),
+        gather_by_bits(attended, "seq", 1),
         out_weight,
         preferred_element_type=jnp.float32,
     )

time: 163 us -> 144 us (0.88)
  blocking collectives: 73.9 us -> 43.3 us
  waiting for transfers between devices: 14.1 us -> 24.7 us
    all_gather x1 -> x0, blocking collectives: 30.6 us -> none  [body(): lax.all_gather(attended, 'seq', axis=1, tiled=True)]
    ppermute x0 -> x3, waiting for transfers between devices: none -> 11 us  [collected_by_bits(): other = lax.ppermute(blocks, axis, [(i, i ^ apart) for i in range(peers)])]
  transfers between devices with their start and end apart: 3 -> 6, of which waited for: 2 -> 5; matrix products, arithmetic and copies ran while one was open for 16% -> 18% of each run, Pallas kernels for 0% -> 0%
where the time goes in v1:
time: 144 us; the launch traced here: 143 us
  blocking collectives  43.3 us (30%)
  local copies, waits for them, and re-layouts  31.6 us (22%)
  waiting for transfers between devices  24.7 us (17%)
  matrix products  20.8 us (14%)
  starting transfers between devices  15.6 us (11%)
  other arithmetic  5.88 us (4%)
    all_gather x1, blocking collectives, body(): everyone = lax.all_gather(queries, 'seq', axis=1, tiled=True)  32.6 us
    reshape x1, local copies, waits for them, and re-layouts, body(): values = cache_values.reshape(blocks, BLK, heads, hdim)  12.9 us
    reshape x1, local copies, waits for them, and re-layouts, body(): keys = cache_keys.reshape(blocks, BLK, heads, hdim)  12.9 us
    ppermute x3, waiting for transfers between devices, collected_by_bits(): other = lax.ppermute(blocks, axis, [(i, i ^ apart) for i in range(peers)])  11 us
    unnamed x1, blocking collectives  10.7 us
    dot_general x1, matrix products, body(): jnp.einsum('sbhd,bthd->bsht', block_query, keys, preferred_element_type=j...  7.37 us
    all_to_all x1, waiting for transfers between devices, body(): lax.all_to_all(tab_acc[None], 'seq', split_axis=2, concat_axis=0, tiled=T...  7.16 us
    all_to_all x1, waiting for transfers between devices, body(): lax.all_to_all(tab_sum[None], 'seq', split_axis=2, concat_axis=0, tiled=T...  6.58 us
  transfers between devices with their start and end apart: 6, of which 5 were waited for; matrix products, arithmetic and copies ran while one was open for 18% of the time, Pallas kernels for 0%

profile of v1, /device:TPU:0, one launch (start us, length us, event | category | flops | bytes accessed | tf_op | source)
XLA Modules:
  0.0 142.9 jit_solution(15047358756827978884)
XLA Ops:
  0.0 0.8 reduce-window.8
  0.8 0.7 iota_add_fusion.1
  1.5 0.9 select_reduce_fusion.2
  2.4 0.2 fusion.72
  2.6 32.6 %all_gather.3 = bf16[2,8,3584]{2,0,1:T(2,128)(2,1)S(1)} all-gather(bf16[2,1,3584]{2,0,1:T(2,128)(2,1)} %param.10), channel_id=1, replica_groups=mesh['seq'=8,'head'=4] {'seq'}, dimensions={1}, use_global_device_ids=true | all-gather | bytes 129024 | tf_op jit(solution)/shard_map/all_gather | solution.py:83
  35.2 0.1 iota_add_fusion
  35.3 0.1 subtract_convert_fusion
  35.4 12.9 %reshape.748 = bf16[8,128,28,128]{3,2,1,0:T(8,128)(2,1)} reshape(bf16[1024,3584]{1,0:T(8,128)(2,1)} %param.13) | data formatting | bytes 14680064 | tf_op jit(solution)/shard_map/reshape | solution.py:94
  48.3 0.8 gather_fusion
  49.1 0.1 bitcast_select_fusion
  49.1 0.0 copy-done.4
  49.2 7.4 %fusion.73 = (f32[8,2,28]{1,2,0:T(8,128)S(1)}, f32[8,2,28,128]{3,1,2,0:T(2,128)S(1)}) fusion(f32[8,2,128]{2,1,0:T(2,128)S(1)} %subtract_convert_fusion, f32[28]{0:T(128)S(1)} %copy-done.4, bf16[8,128,28,128]{3,2,1,0:T(8,128)(2,1)} %reshape.748, bf16[2,8,28,128]{3,1,2,0:T(8,128)(2,1)S(1)} %bitcast_select_fusion), kind=kOutput, calls=%fused_computation.118 | convolution fusion | flops 14908992 | bytes 7694192 | tf_op jit(solution)/shard_map/sbhd,bthd->bsht/dot_general | solution.py:97
  56.5 0.1 copy.153
  56.7 0.1 broadcast_select_fusion.3
  56.7 0.1 copy.154
  56.8 0.1 select_reduce_fusion
  56.9 0.6 copy.218
  57.5 5.5 %all-to-all-start.1 = ((f32[1,2,8,28]{3,1,0,2:T(2,128)}), f32[1,2,8,28]{3,1,0,2:T(2,128)S(1)}, u32[]{:S(2)}, u32[]{:S(2)}) async-start(f32[1,2,8,28]{3,1,0,2:T(2,128)} %bitcast.127.clone.2), calls=%async_computation.1 | async-start | bytes 16384 | tf_op jit(solution)/shard_map/all_to_all | solution.py:132
  63.0 0.0 copy-done
  63.0 1.3 gather_fusion.1
  64.3 0.1 fusion.49
  64.4 0.2 copy.158
  64.5 12.9 %reshape.749 = bf16[8,128,28,128]{3,2,1,0:T(8,128)(2,1)} reshape(bf16[1024,3584]{1,0:T(8,128)(2,1)} %param.14) | data formatting | bytes 14680064 | tf_op jit(solution)/shard_map/reshape | solution.py:95
  77.4 0.6 fusion.29
  78.0 6.6 %fusion.24 = f32[8,2,28,128]{3,1,2,0:T(2,128)S(1)} fusion(bf16[8,128,28,128]{3,2,1,0:T(8,128)(2,1)} %reshape.749, pred[8]{0:T(512)(128)(4,1)S(1)} %fusion.72, f32[8,2,28,128]{3,1,2,0:T(2,128)S(1)} %get-tuple-element.30, f32[8,2,28]{1,2,0:T(8,128)S(1)} %get-tuple-element.29, f32[8,2,28]{1,2,0:T(8,128)S(1)} %copy.158), kind=kOutput, calls=%fused_computation.16 | convolution fusion | flops 14909440 | bytes 7802376 | tf_op jit(solution)/shard_map/bsht,bthd->bshd/dot_general | solution.py:108
  84.6 0.3 convolution_bitcast_fusion
  84.9 0.1 copy.167
  85.0 0.0 copy-done.1
  85.0 0.1 fusion.44
  85.1 0.1 bitcast_reduce_fusion.2
  85.3 0.0 copy-done.2
  85.3 0.1 slice_bitcast_fusion.1
  85.4 0.1 bitcast_reduce_fusion
  85.5 0.1 fusion.42
  85.6 0.2 convolution_bitcast_fusion.1
  85.8 0.9 copy.162
  86.7 0.6 copy.168
  87.3 0.0 all-to-all-done.1
  87.3 6.0 %all-to-all-start.2 = ((f32[1,2,8,28]{3,1,0,2:T(2,128)}), f32[1,2,8,28]{3,1,0,2:T(2,128)S(1)}, u32[]{:S(2)}, u32[]{:S(2)}) async-start(f32[1,2,8,28]{3,1,0,2:T(2,128)} %copy.168), calls=%async_computation.2 | async-start | bytes 16384 | tf_op jit(solution)/shard_map/all_to_all | solution.py:133
  93.3 6.6 %all-to-all-done.2 = f32[1,2,8,28]{3,1,0,2:T(2,128)S(1)} async-done(((f32[1,2,8,28]{3,1,0,2:T(2,128)}), f32[1,2,8,28]{3,1,0,2:T(2,128)S(1)}, u32[]{:S(2)}, u32[]{:S(2)}) %all-to-all-start.2) | async-done | bytes 1824 | tf_op jit(solution)/shard_map/all_to_all | solution.py:133
  99.9 3.6 %all-to-all-start = ((f32[1,2,8,28,128]{4,1,3,0,2:T(2,128)}), f32[1,2,8,28,128]{4,1,3,0,2:T(2,128)S(1)}, u32[]{:S(2)}, u32[]{:S(2)}) async-start(f32[1,2,8,28,128]{4,1,3,0,2:T(2,128)} %copy.162), calls=%async_computation | async-start | bytes 458752 | tf_op jit(solution)/shard_map/all_to_all | solution.py:134
  103.5 0.1 div.33
  103.7 0.1 mul.285
  103.8 0.2 copy.164
  104.0 0.1 copy.165
  104.1 7.2 %all-to-all-done = f32[1,2,8,28,128]{4,1,3,0,2:T(2,128)S(1)} async-done(((f32[1,2,8,28,128]{4,1,3,0,2:T(2,128)}), f32[1,2,8,28,128]{4,1,3,0,2:T(2,128)S(1)}, u32[]{:S(2)}, u32[]{:S(2)}) %all-to-all-start) | async-done | bytes 229408 | tf_op jit(solution)/shard_map/all_to_all | solution.py:134
  111.2 0.3 fusion.27
  111.6 0.0 copy-start.3
  111.6 0.1 fusion.40
  111.7 0.1 collective-permute-start
  111.8 0.1 fusion.41
  111.9 3.6 %collective-permute-done = bf16[1,2,1,3584]{3,1,2,0:T(2,128)(2,1)S(1)} collective-permute-done((bf16[1,2,1,3584]{3,1,2,0:T(2,128)(2,1)S(1)}, bf16[1,2,1,3584]{3,1,2,0:T(2,128)(2,1)S(1)}, u32[]{:S(2)}, u32[]{:S(2)}) %collective-permute-start) | collective-permute-done | bytes 14368 | tf_op jit(solution)/shard_map/ppermute | solution.py:22
  115.6 0.1 collective-permute-start.1
  115.7 3.9 %collective-permute-done.1 = bf16[2,2,1,3584]{3,1,0,2:T(2,128)(2,1)S(1)} collective-permute-done((bf16[2,2,1,3584]{3,1,0,2:T(2,128)(2,1)S(1)}, bf16[2,2,1,3584]{3,1,0,2:T(2,128)(2,1)S(1)}, u32[]{:S(2)}, u32[]{:S(2)}) %collective-permute-start.1) | collective-permute-done | bytes 28704 | tf_op jit(solution)/shard_map/ppermute | solution.py:22
  119.5 0.1 pad_maximum_fusion.1
  119.7 0.5 collective-permute-start.2
  120.1 0.0 copy-done.5
  120.1 0.6 dynamic-slice
  121.4 3.5 %collective-permute-done.2 = bf16[4,2,1,3584]{3,1,0,2:T(2,128)(2,1)S(1)} collective-permute-done((bf16[4,2,1,3584]{3,1,0,2:T(2,128)(2,1)S(1)}, bf16[4,2,1,3584]{3,1,0,2:T(2,128)(2,1)S(1)}, u32[]{:S(2)}, u32[]{:S(2)}) %collective-permute-start.2) | collective-permute-done | bytes 57376 | tf_op jit(solution)/shard_map/ppermute | solution.py:22
  124.9 0.2 pad_maximum_fusion
  125.0 0.1 broadcast_select_fusion
  125.1 6.4 %fusion.6 = bf16[2,8,1792]{2,1,0:T(8,128)(2,1)S(1)} fusion(bf16[3584,1792]{1,0:T(8,128)(2,1)} %param.18, bf16[8,2,1,3584]{3,1,0,2:T(2,128)(2,1)S(1)} %bitcast.151), kind=kOutput, calls=%fused_computation.8 | convolution fusion | flops 205549568 | bytes 13017088 | tf_op jit(solution)/shard_map/srx,xy->sry/dot_general | solution.py:142
  131.5 10.7 %all-reduce.1 = bf16[2,8,1792]{2,1,0:T(8,128)(2,1)S(1)} all-reduce(bf16[2,8,1792]{2,1,0:T(8,128)(2,1)S(1)} %fusion.6), channel_id=2, replica_groups=mesh['seq'=8,'head'=4] {'head'}, use_global_device_ids=true, to_apply=%region_14.15.clone | all-reduce | flops 28672 | bytes 114688
  142.3 0.6 add_convert_fusion
  (31 shorter events, 0.5 us)
Async XLA Ops:
  0.0 49.1 %copy-start.4 = (f32[28]{0:T(128)S(1)}, f32[28]{0:T(128)}, u32[]{:S(2)}) copy-start(f32[28]{0:T(128)} %param.15) | copy-start | bytes 340
  48.3 14.7 %copy-start = (bf16[2,1,3584]{2,0,1:T(2,128)(2,1)S(1)}, bf16[2,1,3584]{2,0,1:T(2,128)(2,1)}, u32[]{:S(2)}) copy-start(bf16[2,1,3584]{2,0,1:T(2,128)(2,1)} %param.10) | copy-start | bytes 43012
  57.5 29.8 %all-to-all-start.1 = ((f32[1,2,8,28]{3,1,0,2:T(2,128)}), f32[1,2,8,28]{3,1,0,2:T(2,128)S(1)}, u32[]{:S(2)}, u32[]{:S(2)}) async-start(f32[1,2,8,28]{3,1,0,2:T(2,128)} %bitcast.127.clone.2), calls=%async_computation.1 | async-start | bytes 16384 | tf_op jit(solution)/shard_map/all_to_all | solution.py:132
  77.4 7.6 %copy-start.1 = (bf16[2,1,3584]{2,0,1:T(2,128)(2,1)S(1)}, bf16[2,1,3584]{2,0,1:T(2,128)(2,1)}, u32[]{:S(2)}) copy-start(bf16[2,1,3584]{2,0,1:T(2,128)(2,1)} %param.11) | copy-start | bytes 43012
  77.4 7.8 %copy-start.2 = (bf16[2,1,3584]{2,0,1:T(2,128)(2,1)S(1)}, bf16[2,1,3584]{2,0,1:T(2,128)(2,1)}, u32[]{:S(2)}) copy-start(bf16[2,1,3584]{2,0,1:T(2,128)(2,1)} %param.12) | copy-start | bytes 43012
  77.4 42.7 %copy-start.5 = (u32[32]{0:T(128)S(1)}, u32[32]{0:T(128)}, u32[]{:S(2)}) copy-start(u32[32]{0:T(128)} %constant.67) | copy-start | bytes 388
  87.3 12.6 %all-to-all-start.2 = ((f32[1,2,8,28]{3,1,0,2:T(2,128)}), f32[1,2,8,28]{3,1,0,2:T(2,128)S(1)}, u32[]{:S(2)}, u32[]{:S(2)}) async-start(f32[1,2,8,28]{3,1,0,2:T(2,128)} %copy.168), calls=%async_computation.2 | async-start | bytes 16384 | tf_op jit(solution)/shard_map/all_to_all | solution.py:133
  99.9 11.3 %all-to-all-start = ((f32[1,2,8,28,128]{4,1,3,0,2:T(2,128)}), f32[1,2,8,28,128]{4,1,3,0,2:T(2,128)S(1)}, u32[]{:S(2)}, u32[]{:S(2)}) async-start(f32[1,2,8,28,128]{4,1,3,0,2:T(2,128)} %copy.162), calls=%async_computation | async-start | bytes 458752 | tf_op jit(solution)/shard_map/all_to_all | solution.py:134
  111.6 30.7 %copy-start.3 = (bf16[2,2,1792]{2,1,0:T(2,128)(2,1)S(1)}, bf16[2,2,1792]{2,1,0:T(2,128)(2,1)}, u32[]{:S(2)}) copy-start(bf16[2,2,1792]{2,1,0:T(2,128)(2,1)} %param.19) | copy-start | bytes 43012
  111.7 3.8 %collective-permute-start = (bf16[1,2,1,3584]{3,1,2,0:T(2,128)(2,1)S(1)}, bf16[1,2,1,3584]{3,1,2,0:T(2,128)(2,1)S(1)}, u32[]{:S(2)}, u32[]{:S(2)}) collective-permute-start(bf16[1,2,1,3584]{3,1,2,0:T(2,128)(2,1)S(1)} %fusion.40), channel_id=1, source_target_pairs={{0,4},{4,0},{8,12},{12,8},{16,20},{20,16},{24,28},{28,24},{1,5},{5... | collective-permute-start | bytes 43016 | tf_op jit(solution)/shard_map/ppermute | solution.py:22
  115.6 3.9 %collective-permute-start.1 = (bf16[2,2,1,3584]{3,1,0,2:T(2,128)(2,1)S(1)}, bf16[2,2,1,3584]{3,1,0,2:T(2,128)(2,1)S(1)}, u32[]{:S(2)}, u32[]{:S(2)}) collective-permute-start(bf16[2,2,1,3584]{3,1,0,2:T(2,128)(2,1)S(1)} %get-tuple-element.18), channel_id=1, source_target_pairs={{0,8},{4,12},{8,0},{12,4},{16,24},{20,28},{24,16},{28,20},{1,9},{5... | collective-permute-start | bytes 86024 | tf_op jit(solution)/shard_map/ppermute | solution.py:22
  119.7 5.2 %collective-permute-start.2 = (bf16[4,2,1,3584]{3,1,0,2:T(2,128)(2,1)S(1)}, bf16[4,2,1,3584]{3,1,0,2:T(2,128)(2,1)S(1)}, u32[]{:S(2)}, u32[]{:S(2)}) collective-permute-start(bf16[4,2,1,3584]{3,1,0,2:T(2,128)(2,1)S(1)} %bitcast.153), channel_id=1, source_target_pairs={{0,16},{4,20},{8,24},{12,28},{16,0},{20,4},{24,8},{28,12},{1,17},{... | collective-permute-start | bytes 172040 | tf_op jit(solution)/shard_map/ppermute | solution.py:22
